TPU v7x, 32 devices: a whole 2x2x4 slice. The times are simulated.
32 devices in a mesh: sector: 4 (over z), axial: 8 (over y, x, core).
Axes of the slice: x: 2, y: 2, z: 4, core: 2. Of those that a mesh axis runs over, the one named last changes fastest.
Arguments:
- kbb: float32 [4096, 64, 64], P(('sector', 'axial')), as said below
- interior: bfloat16 [4096, 256, 64], P(('sector', 'axial')), may hold values from -0.075683594 to 0.075683594
- node_lists: int32 [4096, 64], P(('sector', 'axial')), may hold values from -1 to 63
- owners: int32 [4096, 1], P(('sector', 'axial')), may hold values from 0 to 31; in each aligned block of 128 rows (0 to 127, 128 to 255, ...) at most 8 rows name the same one
- patch_ids: int32 [4096], P(('sector', 'axial')), may hold values from 0 to 63
- counts: int32 [32], P(('sector', 'axial')), may hold values from 96 to 128
- capacity: float32 [131072], P(('sector', 'axial')), may hold values from 0.2 to 2
- links: int32 [2, 512, 2], P(None, ('sector', 'axial')), may hold values from 0 to 63
- conduct: float32 [2, 512, 64], P(None, ('sector', 'axial')), may hold values from 0.5 to 4
- loads: float32 [131072, 128], P(('sector', 'axial')), may hold values from -24 to 24
Outputs:
- current_estimate: float32 [131072, 128], P(('sector', 'axial'))
- remaining_imbalance: float32 [131072, 128], P(('sector', 'axial'))
Inputs may be any that keep to these rules, and one draw needn't show every extreme that they name: `owners`: no owner is named by more than 8 of one device's slots, live or not, and in every draw some owner is named by exactly 8 of some device's slots. The live slots of a device are its first counts slots; the others are padding. `kbb`: the boundary block is symmetric with non-positive entries off the diagonal whose row sums stay under its diagonal.
All inputs are finite; a program needn't handle non-finite values.
Results may differ from a plain program's by a relative error of at most 0.0003.
Values sent between devices are 32-bit elements; how exact they have to be, the bound alone decides.
No kernel may reach another device: no remote copies, remote signals or barrier semaphores. Data moves between devices by JAX's collectives and lax.ppermute only.
A program may use at most 128 MiB of HBM per device.

v0:
```python
import jax
import jax.numpy as jnp
from jax import lax
from jax.sharding import PartitionSpec as P

ITERS = 3
highest = lax.Precision.HIGHEST


def from_behind(array, axis, by):
    length = lax.axis_size(axis)
    return lax.ppermute(array, axis, [(i, (i + by) % length) for i in range(length)])


def shifted(block, axis, distance):
    devices = range(lax.axis_size(axis))
    route = [(i - distance, i) for i in devices if i - distance in devices]
    return lax.ppermute(block, axis, route)


def onehot_rows(index, count):
    return (index[:, None] == jnp.arange(count, dtype=jnp.int32)[None, :]).astype(jnp.float32)


def spread_field(index, values, count):
    return jnp.einsum("lp,lir->pir", onehot_rows(index, count), values, precision=highest)


def spread_flat(index, values, count):
    return jnp.einsum("lp,li->pi", onehot_rows(index, count), values, precision=highest)


def shards(kbb, interior, node_lists, owners, patch_ids, counts, capacity, links, conduct, loads):
    elem_slots, bound_nodes = node_lists.shape
    devices = lax.axis_size("sector") * lax.axis_size("axial")
    slots_each = 2 * elem_slots // devices
    total_slots = devices * slots_each
    points_in_partition, scenario_vectors = loads.shape
    patch_dev = points_in_partition // bound_nodes
    schur = kbb - jnp.einsum("eib,eic->ebc", interior, interior, preferred_element_type=jnp.float32)
    live = (jnp.arange(elem_slots, dtype=jnp.int32) < counts[0]).astype(jnp.int32)
    owner_hot = onehot_rows(owners[:, 0], devices)
    ranks = jnp.sum(jnp.cumsum(owner_hot, axis=0) * owner_hot, axis=1).astype(jnp.int32) - 1
    target = owners[:, 0] * slots_each + ranks
    send_blocks = (
        jnp.zeros((total_slots, bound_nodes, bound_nodes), jnp.float32).at[target].set(schur)
    )
    send_nodes = jnp.full((total_slots, bound_nodes), -1, jnp.int32).at[target].set(node_lists)
    send_patch = jnp.zeros((total_slots,), jnp.int32).at[target].set(patch_ids)
    send_live = jnp.zeros((total_slots,), jnp.int32).at[target].set(live)
    blocks_in, nodes_in, patch_in, live_in = (
        lax.all_to_all(send_blocks, ("sector", "axial"), split_axis=0, concat_axis=0, tiled=True),
        lax.all_to_all(send_nodes, ("sector", "axial"), split_axis=0, concat_axis=0, tiled=True),
        lax.all_to_all(send_patch, ("sector", "axial"), split_axis=0, concat_axis=0, tiled=True),
        lax.all_to_all(send_live, ("sector", "axial"), split_axis=0, concat_axis=0, tiled=True),
    )
    picker = (
        nodes_in[:, :, None] == jnp.arange(bound_nodes, dtype=jnp.int32)[None, None, :]
    ).astype(jnp.float32)
    half = jnp.einsum("rsj,rst->rjt", picker, blocks_in, precision=highest)
    placed = jnp.einsum("rjt,rtk->rjk", half, picker, precision=highest)
    weights = onehot_rows(patch_in, patch_dev) * live_in[:, None].astype(jnp.float32)
    assembled = jnp.einsum("rp,rjk->pjk", weights, placed, precision=highest)
    sector_own = links[0, :, 0]
    sector_far = links[0, :, 1]
    sector_gain = conduct[0]
    axial_own = links[1, :, 0]
    axial_far = links[1, :, 1]
    axial_gain = conduct[1]
    sector_in_far, sector_in_gain = from_behind((sector_far, sector_gain), "sector", 1)
    axial_in_far, axial_in_gain = shifted((axial_far, axial_gain), "axial", 1)
    heat = capacity.reshape(patch_dev, bound_nodes)
    diagonal = heat + jnp.diagonal(assembled, axis1=1, axis2=2)
    diagonal = (
        diagonal
        + spread_flat(sector_own, sector_gain, patch_dev)
        + spread_flat(sector_in_far, sector_in_gain, patch_dev)
    )
    diagonal = (
        diagonal
        + spread_flat(axial_own, axial_gain, patch_dev)
        + spread_flat(axial_in_far, axial_in_gain, patch_dev)
    )

    def precond_sum(remaining_imbalance, precond):
        return lax.psum(jnp.sum(remaining_imbalance * precond, axis=(0, 1)), ("sector", "axial"))

    remaining_imbalance = loads.reshape(patch_dev, bound_nodes, scenario_vectors)
    current_estimate = jnp.zeros_like(remaining_imbalance)
    scale = diagonal[:, :, None]
    precond = remaining_imbalance / scale
    update_vector = precond
    norm_now = precond_sum(remaining_imbalance, precond)
    for sweep in range(ITERS):
        result = heat[:, :, None] * update_vector + jnp.einsum(
            "pij,pjr->pir", assembled, update_vector, precision=highest
        )
        beyond = from_behind(update_vector[sector_in_far], "sector", -1)
        flux = sector_gain[:, :, None] * (update_vector[sector_own] - beyond)
        passed = from_behind(flux, "sector", 1)
        result = (
            result
            + spread_field(sector_own, flux, patch_dev)
            - spread_field(sector_in_far, passed, patch_dev)
        )
        beyond = shifted(update_vector[axial_in_far], "axial", -1)
        flux = axial_gain[:, :, None] * (update_vector[axial_own] - beyond)
        passed = shifted(flux, "axial", 1)
        result = (
            result
            + spread_field(axial_own, flux, patch_dev)
            - spread_field(axial_in_far, passed, patch_dev)
        )
        update_factor = norm_now / lax.psum(
            jnp.sum(update_vector * result, axis=(0, 1)), ("sector", "axial")
        )
        current_estimate = current_estimate + update_factor * update_vector
        remaining_imbalance = remaining_imbalance - update_factor * result
        if sweep + 1 < ITERS:
            precond = remaining_imbalance / scale
            norm_next = precond_sum(remaining_imbalance, precond)
            update_vector = precond + norm_next / norm_now * update_vector
            norm_now = norm_next
    return (
        current_estimate.reshape(points_in_partition, scenario_vectors),
        remaining_imbalance.reshape(points_in_partition, scenario_vectors),
    )


def solution(mesh):
    placed = (
        P(("sector", "axial"), None, None),
        P(("sector", "axial"), None, None),
        P(("sector", "axial"), None),
        P(("sector", "axial"), None),
        P(("sector", "axial")),
        P(("sector", "axial")),
        P(("sector", "axial")),
        P(None, ("sector", "axial"), None),
        P(None, ("sector", "axial"), None),
        P(("sector", "axial"), None),
    )
    return jax.shard_map(
        shards,
        mesh=mesh,
        in_specs=placed,
        out_specs=(P(("sector", "axial"), None), P(("sector", "axial"), None)),
        check_vma=False,
    )
```

profile of v0, /device:TPU:10, one launch (start us, length us, event | category | flops | bytes accessed | tf_op | source)
XLA Modules:
  0.0 622.8 jit_solution(7202846408577687185)
XLA Ops:
  5.4 6.0 all-to-all-start.1
  13.2 3.1 all-to-all-done.1
  16.4 4.6 all-to-all-start
  21.0 5.6 copy.75
  28.3 5.9 all-to-all-start.2
  34.2 7.9 %convolution_subtract_fusion = f32[128,64,64]{2,1,0:T(8,128)} fusion(f32[128,64,64]{2,1,0:T(8,128)} %copy.75, bf16[128,256,64]{1,2,0:T(8,128)(2,1)} %param.11), kind=kOutput, calls=%fused_computation.25 | convolution fusion | flops 268959744 | bytes 8388608 | tf_op jit(solution)/shard_map/eib,eic->ebc/dot_general | solution.py:40
  42.1 4.3 broadcast_in_dim.11
  46.4 19.3 %scatter_fusion = f32[256,64,64]{2,1,0:T(8,128)} fusion(f32[256,64,64]{2,1,0:T(8,128)} %broadcast_in_dim.11, s32[128]{0:T(128)S(1)} %fusion.85, f32[128,64,64]{2,1,0:T(8,128)} %convolution_subtract_fusion), kind=kCustom, calls=%fused_computation.16 | custom fusion | bytes 6291968 | tf_op jit(solution)/shard_map/scatter | solution.py:46
  65.7 9.8 %reshape.288 = f32[32,1,32768]{2,1,0:T(1,128)} reshape(f32[256,64,64]{2,1,0:T(8,128)} %scatter_fusion) | data formatting | bytes 8388608
  75.6 5.9 all-to-all-start.3
  83.0 1.5 collective-permute-start
  84.6 1.9 collective-permute-start.3
  86.5 3.5 collective-permute-start.2
  90.4 13.4 %collective-permute-done.2 = s32[16]{0:T(128)S(1)} collective-permute-done((s32[16]{0:T(128)S(1)}, s32[16]{0:T(128)S(1)}, u32[]{:S(2)}, u32[]{:S(2)}) %collective-permute-start.2) | collective-permute-done | bytes 96 | tf_op jit(solution)/shard_map/ppermute | solution.py:18
  106.6 65.6 %all-to-all-done.3 = f32[32,1,32768]{2,1,0:T(1,128)} async-done(((f32[32,1,32768]{2,1,0:T(1,128)}), f32[32,1,32768]{2,1,0:T(1,128)}, u32[]{:S(2)}, u32[]{:S(2)}) %all-to-all-start.3) | async-done | bytes 4194336 | tf_op jit(solution)/shard_map/all_to_all | solution.py:52
  172.7 13.7 %reduce.9 = f32[32,32768]{1,0:T(8,128)} reduce(f32[32,1,32768]{2,1,0:T(1,128)} %all-to-all-done.3, f32[]{:T(128)} %broadcast.166), dimensions={1}, to_apply=%all_to_all.27.reduce_sub_computation | reduce | bytes 8388612 | tf_op jit(solution)/shard_map/all_to_all | solution.py:52
  186.5 7.4 %reshape.289 = f32[256,64,64]{2,1,0:T(8,128)} reshape(f32[32,32768]{1,0:T(8,128)} %reduce.9) | data formatting | bytes 8388608
  193.8 11.8 %fusion.3 = f32[256,64,64]{2,1,0:T(8,128)S(1)} fusion(f32[256,64,64]{2,1,0:T(8,128)} %reshape.289, s32[256,64]{1,0:T(8,128)S(1)} %bitcast.83), kind=kOutput, calls=%fused_computation.21 | convolution fusion | flops 806354944 | bytes 8454144 | tf_op jit(solution)/shard_map/rsj,rst->rjt/dot_general | solution.py:60
  205.7 8.2 %fusion.2 = f32[256,64,64]{2,1,0:T(8,128)S(1)} fusion(f32[256,64,64]{2,1,0:T(8,128)S(1)} %fusion.3, s32[256,64]{1,0:T(8,128)S(1)} %bitcast.84), kind=kOutput, calls=%fused_computation.20 | convolution fusion | flops 806354944 | bytes 8454144 | tf_op jit(solution)/shard_map/rjt,rtk->rjk/dot_general | solution.py:61
  213.8 11.0 %fusion = f32[64,64,64]{2,0,1:T(8,128)} fusion(f32[256,64,64]{2,1,0:T(8,128)S(1)} %fusion.2, f32[256]{0:T(256)S(1)} %convert_element_type.50, s32[256]{0:T(256)S(1)} %eq.56), kind=kOutput, calls=%fused_computation.17 | convolution fusion | flops 805339136 | bytes 5244928 | tf_op jit(solution)/shard_map/rp,rjk->pjk/dot_general | solution.py:63
  224.9 3.0 copy.78
  227.9 1.6 gather_fusion
  230.5 1.7 broadcast_divide_fusion
  232.2 3.0 gather_fusion.4
  235.1 2.8 collective-permute-start.6
  238.0 2.2 gather_fusion.3
  240.2 2.2 gather_fusion.1
  242.4 3.0 gather_fusion.2
  245.4 2.6 collective-permute-start.4
  249.9 2.1 collective-permute-start.7
  252.1 8.1 %collective-permute-done.4 = f32[16,64,128]{2,1,0:T(8,128)S(1)} collective-permute-done((f32[16,64,128]{2,1,0:T(8,128)}, f32[16,64,128]{2,1,0:T(8,128)S(1)}, u32[]{:S(2)}, u32[]{:S(2)}) %collective-permute-start.4) | collective-permute-done | bytes 524320 | tf_op jit(solution)/shard_map/ppermute | solution.py:12
  260.4 1.7 collective-permute-start.5
  265.6 9.5 %collective-permute-done.5 = f32[16,64,128]{2,1,0:T(8,128)S(1)} collective-permute-done((f32[16,64,128]{2,1,0:T(8,128)S(1)}, f32[16,64,128]{2,1,0:T(8,128)S(1)}, u32[]{:S(2)}, u32[]{:S(2)}) %collective-permute-start.5) | collective-permute-done | bytes 524320 | tf_op jit(solution)/shard_map/ppermute | solution.py:12
  276.2 13.9 %multiply_reduce_fusion.4 = (f32[128]{0:T(128)S(1)}, f32[64,64,128]{2,1,0:T(8,128)}) fusion(f32[64,64,128]{2,1,0:T(8,128)S(1)} %copy-done.6, f32[64,64,128]{2,0,1:T(8,128)S(1)} %fusion.36, f32[64,64,128]{2,0,1:T(8,128)S(1)} %fusion.38, f32[64,64,128]{2,0,1:T(8,128)S(1)} %fusion.40, f32[64,64,128]{2,0,1:T(8,128)S(1)} %fusion.42, ...), kind=kOutput, calls=%fused_computation.48 | convolution fusion | flops 406847360 | bytes 13648384 | tf_op jit(solution)/shard_map/pij,pjr->pir/dot_general | solution.py:95
  290.1 43.9 %all-reduce = (f32[128]{0:T(128)S(1)}, f32[128]{0:T(128)S(1)}) all-reduce(f32[128]{0:T(128)S(1)} %fusion.6, f32[128]{0:T(128)S(1)} %get-tuple-element.18), channel_id=1, replica_groups=mesh['sector'=4,'axial'=8] {'sector','axial'}, use_global_device_ids=true, to_apply=%region_7.8 | all-reduce | flops 256 | bytes 2048 | tf_op jit(solution)/shard_map/psum | solution.py:86
  334.1 2.9 multiply_reduce_fusion.3
  336.9 38.0 %psum.44 = f32[128]{0:T(128)S(1)} all-reduce(f32[128]{0:T(128)S(1)} %get-tuple-element.6), channel_id=1, replica_groups=mesh['sector'=4,'axial'=8] {'sector','axial'}, use_global_device_ids=true, to_apply=%region_11.12 | all-reduce | flops 128 | bytes 1024 | tf_op jit(solution)/shard_map/psum | solution.py:86
  374.9 3.1 multiply_add_fusion.2
  378.0 3.0 gather_fusion.8
  381.0 1.9 collective-permute-start.10
  382.9 3.0 gather_fusion.6
  385.8 2.1 collective-permute-start.8
  387.9 2.2 gather_fusion.7
  390.1 2.2 gather_fusion.5
  393.5 2.1 collective-permute-start.11
  395.7 4.8 collective-permute-done.8
  406.4 9.3 %collective-permute-done.9 = f32[16,64,128]{2,1,0:T(8,128)S(1)} collective-permute-done((f32[16,64,128]{2,1,0:T(8,128)S(1)}, f32[16,64,128]{2,1,0:T(8,128)S(1)}, u32[]{:S(2)}, u32[]{:S(2)}) %collective-permute-start.9) | collective-permute-done | bytes 524320 | tf_op jit(solution)/shard_map/ppermute | solution.py:12
  416.9 13.9 %multiply_reduce_fusion.2 = (f32[128]{0:T(128)S(1)}, f32[64,64,128]{2,1,0:T(8,128)}) fusion(f32[64,64,128]{2,1,0:T(8,128)S(1)} %copy-done.1, f32[64,64,128]{2,0,1:T(8,128)S(1)} %fusion.28, f32[64,64,128]{2,0,1:T(8,128)S(1)} %fusion.30, f32[64,64,128]{2,0,1:T(8,128)S(1)} %fusion.32, f32[64,64,128]{2,0,1:T(8,128)S(1)} %fusion.34, ...), kind=kOutput, calls=%fused_computation.44 | convolution fusion | flops 406847360 | bytes 13648384 | tf_op jit(solution)/shard_map/pij,pjr->pir/dot_general | solution.py:95
  430.8 44.4 %psum.45 = f32[128]{0:T(128)S(1)} all-reduce(f32[128]{0:T(128)S(1)} %get-tuple-element.20), channel_id=1, replica_groups=mesh['sector'=4,'axial'=8] {'sector','axial'}, use_global_device_ids=true, to_apply=%region_13.14 | all-reduce | flops 128 | bytes 1024 | tf_op jit(solution)/shard_map/psum | solution.py:114
  475.1 3.5 multiply_reduce_fusion.1
  478.6 38.0 %psum.46 = f32[128]{0:T(128)S(1)} all-reduce(f32[128]{0:T(128)S(1)} %get-tuple-element.4), channel_id=1, replica_groups=mesh['sector'=4,'axial'=8] {'sector','axial'}, use_global_device_ids=true, to_apply=%region_15.16 | all-reduce | flops 128 | bytes 1024 | tf_op jit(solution)/shard_map/psum | solution.py:86
  516.6 3.6 multiply_add_fusion.1
  520.1 3.0 gather_fusion.12
  523.1 1.9 collective-permute-start.14
  525.0 3.0 gather_fusion.10
  528.0 2.1 collective-permute-start.12
  530.1 2.2 gather_fusion.11
  532.3 2.2 gather_fusion.9
  535.7 2.1 collective-permute-start.15
  537.9 4.8 collective-permute-done.12
  548.6 9.3 %collective-permute-done.13 = f32[16,64,128]{2,1,0:T(8,128)S(1)} collective-permute-done((f32[16,64,128]{2,1,0:T(8,128)S(1)}, f32[16,64,128]{2,1,0:T(8,128)S(1)}, u32[]{:S(2)}, u32[]{:S(2)}) %collective-permute-start.13) | collective-permute-done | bytes 524320 | tf_op jit(solution)/shard_map/ppermute | solution.py:12
  559.0 13.9 %multiply_reduce_fusion = (f32[128]{0:T(128)S(1)}, f32[64,64,128]{2,1,0:T(8,128)}) fusion(f32[64,64,128]{2,1,0:T(8,128)S(1)} %copy-done.5, f32[64,64,128]{2,0,1:T(8,128)S(1)} %fusion.20, f32[64,64,128]{2,0,1:T(8,128)S(1)} %fusion.22, f32[64,64,128]{2,0,1:T(8,128)S(1)} %fusion.24, f32[64,64,128]{2,0,1:T(8,128)S(1)} %fusion.26, ...), kind=kOutput, calls=%fused_computation.40 | convolution fusion | flops 406847360 | bytes 13648384 | tf_op jit(solution)/shard_map/pij,pjr->pir/dot_general | solution.py:95
  572.9 44.1 %psum.47 = f32[128]{0:T(128)S(1)} all-reduce(f32[128]{0:T(128)S(1)} %get-tuple-element.22), channel_id=1, replica_groups=mesh['sector'=4,'axial'=8] {'sector','axial'}, use_global_device_ids=true, to_apply=%region_17.18 | all-reduce | flops 128 | bytes 1024 | tf_op jit(solution)/shard_map/psum | solution.py:114
  617.1 5.3 multiply_subtract_fusion
  (98 shorter events, 37.4 us)
Async XLA Ops:
  5.4 11.0 %all-to-all-start.1 = ((s32[32,8,1]{1,2,0:T(1,128)}), s32[32,8,1]{1,2,0:T(1,128)S(1)}, u32[]{:S(2)}, u32[]{:S(2)}) async-start(s32[32,8,1]{1,2,0:T(1,128)} %bitcast.5), calls=%async_computation.1 | async-start | bytes 32768 | tf_op jit(solution)/shard_map/all_to_all | solution.py:55
  16.4 12.0 %all-to-all-start = ((s32[32,8,1]{1,2,0:T(1,128)}), s32[32,8,1]{1,2,0:T(1,128)S(1)}, u32[]{:S(2)}, u32[]{:S(2)}) async-start(s32[32,8,1]{1,2,0:T(1,128)} %bitcast.3), calls=%async_computation | async-start | bytes 32768 | tf_op jit(solution)/shard_map/all_to_all | solution.py:54
  21.0 5.6 copy-start.8
  28.3 47.2 %all-to-all-start.2 = ((s32[32,1,512]{2,1,0:T(1,128)}), s32[32,1,512]{2,1,0:T(1,128)S(1)}, u32[]{:S(2)}, u32[]{:S(2)}) async-start(s32[32,1,512]{2,1,0:T(1,128)} %reshape.290), calls=%async_computation.2 | async-start | bytes 131072 | tf_op jit(solution)/shard_map/all_to_all | solution.py:53
  75.5 5.9 copy-start.7
  75.5 7.5 %copy-start.10 = (s32[2,16,2]{1,2,0:T(2,128)S(1)}, s32[2,16,2]{1,2,0:T(2,128)}, u32[]{:S(2)}) copy-start(s32[2,16,2]{1,2,0:T(2,128)} %param.17) | copy-start | bytes 772
  75.5 14.8 %copy-start.9 = (f32[4096]{0:T(1024)S(1)}, f32[4096]{0:T(1024)}, u32[]{:S(2)}) copy-start(f32[4096]{0:T(1024)} %param.16) | copy-start | bytes 49156
  75.6 96.7 %all-to-all-start.3 = ((f32[32,1,32768]{2,1,0:T(1,128)}), f32[32,1,32768]{2,1,0:T(1,128)}, u32[]{:S(2)}, u32[]{:S(2)}) async-start(f32[32,1,32768]{2,1,0:T(1,128)} %reshape.288), calls=%async_computation.3 | async-start | bytes 8388608 | tf_op jit(solution)/shard_map/all_to_all | solution.py:52
  81.5 148.4 %collective-permute-start.1 = (f32[16,64]{1,0:T(8,128)S(1)}, f32[16,64]{1,0:T(8,128)S(1)}, u32[]{:S(2)}, u32[]{:S(2)}) collective-permute-start(f32[16,64]{1,0:T(8,128)S(1)} %get-tuple-element.9), channel_id=1, source_target_pairs={{0,8},{8,16},{16,24},{24,0},{1,9},{9,17},{17,25},{25,1},{2,10},{10... | collective-permute-start | bytes 12296 | tf_op jit(solution)/shard_map/ppermute | solution.py:12
  83.0 146.8 %collective-permute-start = (s32[16]{0:T(128)S(1)}, s32[16]{0:T(128)S(1)}, u32[]{:S(2)}, u32[]{:S(2)}) collective-permute-start(s32[16]{0:T(128)S(1)} %get-tuple-element.13), channel_id=1, source_target_pairs={{0,8},{8,16},{16,24},{24,0},{1,9},{9,17},{17,25},{25,1},{2,10},{10... | collective-permute-start | bytes 200 | tf_op jit(solution)/shard_map/ppermute | solution.py:12
  84.6 145.6 %collective-permute-start.3 = (f32[16,64]{1,0:T(8,128)S(1)}, f32[16,64]{1,0:T(8,128)S(1)}, u32[]{:S(2)}, u32[]{:S(2)}) collective-permute-start(f32[16,64]{1,0:T(8,128)S(1)} %get-tuple-element.8), channel_id=1, source_target_pairs={{0,1},{1,2},{2,3},{3,4},{4,5},{5,6},{6,7},{8,9},{9,10},{10,11},{11... | collective-permute-start | bytes 12296 | tf_op jit(solution)/shard_map/ppermute | solution.py:18
  86.5 17.3 %collective-permute-start.2 = (s32[16]{0:T(128)S(1)}, s32[16]{0:T(128)S(1)}, u32[]{:S(2)}, u32[]{:S(2)}) collective-permute-start(s32[16]{0:T(128)S(1)} %get-tuple-element.12), channel_id=1, source_target_pairs={{0,1},{1,2},{2,3},{3,4},{4,5},{5,6},{6,7},{8,9},{9,10},{10,11},{11... | collective-permute-start | bytes 200 | tf_op jit(solution)/shard_map/ppermute | solution.py:18
  224.9 5.6 copy-start
  235.1 13.5 %collective-permute-start.6 = (f32[16,64,128]{2,1,0:T(8,128)}, f32[16,64,128]{2,1,0:T(8,128)}, u32[]{:S(2)}, u32[]{:S(2)}) collective-permute-start(f32[16,64,128]{2,1,0:T(8,128)} %gather_fusion.4), channel_id=1, source_target_pairs={{1,0},{2,1},{3,2},{4,3},{5,4},{6,5},{7,6},{9,8},{10,9},{11,10},{12... | collective-permute-start | bytes 1572872 | tf_op jit(solution)/shard_map/ppermute | solution.py:18
  245.4 14.7 %collective-permute-start.4 = (f32[16,64,128]{2,1,0:T(8,128)}, f32[16,64,128]{2,1,0:T(8,128)S(1)}, u32[]{:S(2)}, u32[]{:S(2)}) collective-permute-start(f32[16,64,128]{2,1,0:T(8,128)} %gather_fusion.2), channel_id=1, source_target_pairs={{0,24},{8,0},{16,8},{24,16},{1,25},{9,1},{17,9},{25,17},{2,26},{10... | collective-permute-start | bytes 1572872 | tf_op jit(solution)/shard_map/ppermute | solution.py:12
  249.9 14.5 %collective-permute-start.7 = (f32[16,64,128]{2,1,0:T(8,128)S(1)}, f32[16,64,128]{2,1,0:T(8,128)S(1)}, u32[]{:S(2)}, u32[]{:S(2)}) collective-permute-start(f32[16,64,128]{2,1,0:T(8,128)S(1)} %subtract_multiply_fusion.4), channel_id=1, source_target_pairs={{0,1},{1,2},{2,3},{3,4},{4,5},{5,6},{6,7},{8,9},{9,10},{10,11},{11... | collective-permute-start | bytes 1572872 | tf_op jit(solution)/shard_map/ppermute | solution.py:18
  260.4 14.7 %collective-permute-start.5 = (f32[16,64,128]{2,1,0:T(8,128)S(1)}, f32[16,64,128]{2,1,0:T(8,128)S(1)}, u32[]{:S(2)}, u32[]{:S(2)}) collective-permute-start(f32[16,64,128]{2,1,0:T(8,128)S(1)} %subtract_multiply_fusion.5), channel_id=1, source_target_pairs={{0,8},{8,16},{16,24},{24,0},{1,9},{9,17},{17,25},{25,1},{2,10},{10... | collective-permute-start | bytes 1572872 | tf_op jit(solution)/shard_map/ppermute | solution.py:12
  264.4 11.9 %copy-start.2 = (f32[64,64,64]{2,0,1:T(8,128)S(1)}, f32[64,64,64]{2,0,1:T(8,128)}, u32[]{:S(2)}) copy-start(f32[64,64,64]{2,0,1:T(8,128)} %fusion) | copy-start | bytes 3145732
  264.4 11.9 %copy-start.6 = (f32[64,64,128]{2,1,0:T(8,128)S(1)}, f32[64,64,128]{2,1,0:T(8,128)}, u32[]{:S(2)}) copy-start(f32[64,64,128]{2,1,0:T(8,128)} %broadcast_divide_fusion) | copy-start | bytes 6291460
  381.0 11.3 %collective-permute-start.10 = (f32[16,64,128]{2,1,0:T(8,128)}, f32[16,64,128]{2,1,0:T(8,128)}, u32[]{:S(2)}, u32[]{:S(2)}) collective-permute-start(f32[16,64,128]{2,1,0:T(8,128)} %gather_fusion.8), channel_id=1, source_target_pairs={{1,0},{2,1},{3,2},{4,3},{5,4},{6,5},{7,6},{9,8},{10,9},{11,10},{12... | collective-permute-start | bytes 1572872 | tf_op jit(solution)/shard_map/ppermute | solution.py:18
  385.8 14.6 %collective-permute-start.8 = (f32[16,64,128]{2,1,0:T(8,128)}, f32[16,64,128]{2,1,0:T(8,128)}, u32[]{:S(2)}, u32[]{:S(2)}) collective-permute-start(f32[16,64,128]{2,1,0:T(8,128)} %gather_fusion.6), channel_id=1, source_target_pairs={{0,24},{8,0},{16,8},{24,16},{1,25},{9,1},{17,9},{25,17},{2,26},{10... | collective-permute-start | bytes 1572872 | tf_op jit(solution)/shard_map/ppermute | solution.py:12
  393.5 11.7 %collective-permute-start.11 = (f32[16,64,128]{2,1,0:T(8,128)S(1)}, f32[16,64,128]{2,1,0:T(8,128)S(1)}, u32[]{:S(2)}, u32[]{:S(2)}) collective-permute-start(f32[16,64,128]{2,1,0:T(8,128)S(1)} %subtract_multiply_fusion.2), channel_id=1, source_target_pairs={{0,1},{1,2},{2,3},{3,4},{4,5},{5,6},{6,7},{8,9},{9,10},{10,11},{11... | collective-permute-start | bytes 1572872 | tf_op jit(solution)/shard_map/ppermute | solution.py:18
  401.7 14.0 %collective-permute-start.9 = (f32[16,64,128]{2,1,0:T(8,128)S(1)}, f32[16,64,128]{2,1,0:T(8,128)S(1)}, u32[]{:S(2)}, u32[]{:S(2)}) collective-permute-start(f32[16,64,128]{2,1,0:T(8,128)S(1)} %subtract_multiply_fusion.3), channel_id=1, source_target_pairs={{0,8},{8,16},{16,24},{24,0},{1,9},{9,17},{17,25},{25,1},{2,10},{10... | collective-permute-start | bytes 1572872 | tf_op jit(solution)/shard_map/ppermute | solution.py:12
  405.2 11.7 %copy-start.1 = (f32[64,64,128]{2,1,0:T(8,128)S(1)}, f32[64,64,128]{2,1,0:T(8,128)}, u32[]{:S(2)}) copy-start(f32[64,64,128]{2,1,0:T(8,128)} %multiply_add_fusion.2) | copy-start | bytes 6291460
  405.2 11.7 %copy-start.3 = (f32[64,64,64]{2,0,1:T(8,128)S(1)}, f32[64,64,64]{2,0,1:T(8,128)}, u32[]{:S(2)}) copy-start(f32[64,64,64]{2,0,1:T(8,128)} %fusion) | copy-start | bytes 3145732
  523.1 11.4 %collective-permute-start.14 = (f32[16,64,128]{2,1,0:T(8,128)}, f32[16,64,128]{2,1,0:T(8,128)}, u32[]{:S(2)}, u32[]{:S(2)}) collective-permute-start(f32[16,64,128]{2,1,0:T(8,128)} %gather_fusion.12), channel_id=1, source_target_pairs={{1,0},{2,1},{3,2},{4,3},{5,4},{6,5},{7,6},{9,8},{10,9},{11,10},{12... | collective-permute-start | bytes 1572872 | tf_op jit(solution)/shard_map/ppermute | solution.py:18
  528.0 14.6 %collective-permute-start.12 = (f32[16,64,128]{2,1,0:T(8,128)}, f32[16,64,128]{2,1,0:T(8,128)}, u32[]{:S(2)}, u32[]{:S(2)}) collective-permute-start(f32[16,64,128]{2,1,0:T(8,128)} %gather_fusion.10), channel_id=1, source_target_pairs={{0,24},{8,0},{16,8},{24,16},{1,25},{9,1},{17,9},{25,17},{2,26},{10... | collective-permute-start | bytes 1572872 | tf_op jit(solution)/shard_map/ppermute | solution.py:12
  535.7 11.7 %collective-permute-start.15 = (f32[16,64,128]{2,1,0:T(8,128)S(1)}, f32[16,64,128]{2,1,0:T(8,128)S(1)}, u32[]{:S(2)}, u32[]{:S(2)}) collective-permute-start(f32[16,64,128]{2,1,0:T(8,128)S(1)} %subtract_multiply_fusion), channel_id=1, source_target_pairs={{0,1},{1,2},{2,3},{3,4},{4,5},{5,6},{6,7},{8,9},{9,10},{10,11},{11... | collective-permute-start | bytes 1572872 | tf_op jit(solution)/shard_map/ppermute | solution.py:18
  543.9 14.0 %collective-permute-start.13 = (f32[16,64,128]{2,1,0:T(8,128)S(1)}, f32[16,64,128]{2,1,0:T(8,128)S(1)}, u32[]{:S(2)}, u32[]{:S(2)}) collective-permute-start(f32[16,64,128]{2,1,0:T(8,128)S(1)} %subtract_multiply_fusion.1), channel_id=1, source_target_pairs={{0,8},{8,16},{16,24},{24,0},{1,9},{9,17},{17,25},{25,1},{2,10},{10... | collective-permute-start | bytes 1572872 | tf_op jit(solution)/shard_map/ppermute | solution.py:12
  547.4 11.6 %copy-start.4 = (f32[64,64,64]{2,0,1:T(8,128)S(1)}, f32[64,64,64]{2,0,1:T(8,128)}, u32[]{:S(2)}) copy-start(f32[64,64,64]{2,0,1:T(8,128)} %fusion) | copy-start | bytes 3145732
  547.4 11.6 %copy-start.5 = (f32[64,64,128]{2,1,0:T(8,128)S(1)}, f32[64,64,128]{2,1,0:T(8,128)}, u32[]{:S(2)}) copy-start(f32[64,64,128]{2,1,0:T(8,128)} %multiply_add_fusion.1) | copy-start | bytes 6291460
where the time goes:
time: 633 us; the launch traced here: 623 us
  blocking collectives  208 us (33%)
  waiting for transfers between devices  128 us (20%)
  matrix products  95.7 us (15%)
  local copies, waits for them, and re-layouts  89.1 us (14%)
  starting transfers between devices  54.6 us (9%)
  other arithmetic  44.9 us (7%)
    psum x3, blocking collectives, precond_sum(): lax.psum(jnp.sum(remaining_imbalance * precond, axis=(0, 1)), ('sector',...  120 us
    psum x2, blocking collectives, shards(): lax.psum(jnp.sum(update_vector * result, axis=(0, 1)), ('sector', 'axial'))  88.5 us
    all_to_all x1, waiting for transfers between devices, shards(): lax.all_to_all(send_blocks, ('sector', 'axial'), split_axis=0, concat_axi...  65.6 us
    ppermute x8, waiting for transfers between devices, from_behind(): lax.ppermute(array, axis, [(i, (i + by) % length) for i in range(length)])  45.7 us
    dot_general x3, matrix products, shards(): jnp.einsum('pij,pjr->pir', assembled, update_vector, precision=highest)  41.7 us
    unnamed x28, local copies, waits for them, and re-layouts  23.7 us
    scatter x1, local copies, waits for them, and re-layouts, shards(): jnp.zeros((total_slots, bound_nodes, bound_nodes), jnp.float32).at[target]  19.3 us
    ppermute x8, starting transfers between devices, shifted(): return lax.ppermute(block, axis, route)  18.4 us
  transfers between devices with their start and end apart: 20, of which 9 were waited for; matrix products, arithmetic and copies ran while one was open for 24% of the time, Pallas kernels for 0%

commit v1 on v0

--- a/solution.py
+++ b/solution.py
@@ -5,6 +5,11 @@
 
 ITERS = 3
 highest = lax.Precision.HIGHEST
+
+
+def by_each_axis(x, inner_axis, outer_axis):
+    inner = lax.psum(x, inner_axis)
+    return lax.psum(inner, outer_axis)
 
 
 def from_behind(array, axis, by):
@@ -111,8 +116,8 @@
             + spread_field(axial_own, flux, patch_dev)
             - spread_field(axial_in_far, passed, patch_dev)
         )
-        update_factor = norm_now / lax.psum(
-            jnp.sum(update_vector * result, axis=(0, 1)), ("sector", "axial")
+        update_factor = norm_now / by_each_axis(
+            jnp.sum(update_vector * result, axis=(0, 1)), "axial", "sector"
         )
         current_estimate = current_estimate + update_factor * update_vector
         remaining_imbalance = remaining_imbalance - update_factor * result

time: 633 us -> 612 us (0.967)
  the two profiles are of different devices: /device:TPU:10 before, /device:TPU:0 now
where the time goes in v1:
time: 612 us; the launch traced here: 602 us
  blocking collectives  189 us (31%)
  waiting for transfers between devices  128 us (21%)
  matrix products  95.9 us (16%)
  local copies, waits for them, and re-layouts  89.2 us (15%)
  starting transfers between devices  51.2 us (8%)
  other arithmetic  45.9 us (8%)
    psum x3, blocking collectives, precond_sum(): lax.psum(jnp.sum(remaining_imbalance * precond, axis=(0, 1)), ('sector',...  119 us
    all_to_all x1, waiting for transfers between devices, shards(): lax.all_to_all(send_blocks, ('sector', 'axial'), split_axis=0, concat_axi...  81.8 us
    psum x3, blocking collectives, by_each_axis(): inner = lax.psum(x, inner_axis)  43.2 us
    dot_general x3, matrix products, shards(): jnp.einsum('pij,pjr->pir', assembled, update_vector, precision=highest)  41.7 us
    ppermute x8, waiting for transfers between devices, from_behind(): lax.ppermute(array, axis, [(i, (i + by) % length) for i in range(length)])  41.1 us
    psum x3, blocking collectives, by_each_axis(): return lax.psum(inner, outer_axis)  27.3 us
    unnamed x28, local copies, waits for them, and re-layouts  23.7 us
    scatter x1, local copies, waits for them, and re-layouts, shards(): jnp.zeros((total_slots, bound_nodes, bound_nodes), jnp.float32).at[target]  19.4 us
  transfers between devices with their start and end apart: 20, of which 8 were waited for; matrix products, arithmetic and copies ran while one was open for 25% of the time, Pallas kernels for 0%

profile of v1, /device:TPU:0, one launch (start us, length us, event | category | flops | bytes accessed | tf_op | source)
XLA Modules:
  0.0 602.0 jit_solution(2789653582618781558)
XLA Ops:
  5.4 7.3 %all-to-all-start.1 = ((s32[32,8,1]{1,2,0:T(1,128)}), s32[32,8,1]{1,2,0:T(1,128)S(1)}, u32[]{:S(2)}, u32[]{:S(2)}) async-start(s32[32,8,1]{1,2,0:T(1,128)} %bitcast.5), calls=%async_computation.1 | async-start | bytes 32768 | tf_op jit(solution)/shard_map/all_to_all | solution.py:60
  14.5 5.3 all-to-all-done.1
  19.8 2.5 all-to-all-start
  22.3 5.6 copy.75
  29.7 5.8 all-to-all-start.2
  35.5 7.9 %convolution_subtract_fusion = f32[128,64,64]{2,1,0:T(8,128)} fusion(f32[128,64,64]{2,1,0:T(8,128)} %copy.75, bf16[128,256,64]{1,2,0:T(8,128)(2,1)} %param.11), kind=kOutput, calls=%fused_computation.25 | convolution fusion | flops 268959744 | bytes 8388608 | tf_op jit(solution)/shard_map/eib,eic->ebc/dot_general | solution.py:45
  43.4 4.3 broadcast_in_dim.11
  47.7 19.4 %scatter_fusion = f32[256,64,64]{2,1,0:T(8,128)} fusion(f32[256,64,64]{2,1,0:T(8,128)} %broadcast_in_dim.11, s32[128]{0:T(128)S(1)} %fusion.85, f32[128,64,64]{2,1,0:T(8,128)} %convolution_subtract_fusion), kind=kCustom, calls=%fused_computation.16 | custom fusion | bytes 6291968 | tf_op jit(solution)/shard_map/scatter | solution.py:51
  67.1 9.8 %reshape.288 = f32[32,1,32768]{2,1,0:T(1,128)} reshape(f32[256,64,64]{2,1,0:T(8,128)} %scatter_fusion) | data formatting | bytes 8388608
  76.9 5.9 all-to-all-start.3
  82.9 1.7 collective-permute-start.1
  84.6 1.5 collective-permute-start
  86.1 1.5 collective-permute-start.3
  87.6 3.9 collective-permute-start.2
  95.1 81.8 %all-to-all-done.3 = f32[32,1,32768]{2,1,0:T(1,128)} async-done(((f32[32,1,32768]{2,1,0:T(1,128)}), f32[32,1,32768]{2,1,0:T(1,128)}, u32[]{:S(2)}, u32[]{:S(2)}) %all-to-all-start.3) | async-done | bytes 4194336 | tf_op jit(solution)/shard_map/all_to_all | solution.py:57
  177.4 13.7 %reduce.9 = f32[32,32768]{1,0:T(8,128)} reduce(f32[32,1,32768]{2,1,0:T(1,128)} %all-to-all-done.3, f32[]{:T(128)} %broadcast.166), dimensions={1}, to_apply=%all_to_all.27.reduce_sub_computation | reduce | bytes 8388612 | tf_op jit(solution)/shard_map/all_to_all | solution.py:57
  191.1 7.4 %reshape.289 = f32[256,64,64]{2,1,0:T(8,128)} reshape(f32[32,32768]{1,0:T(8,128)} %reduce.9) | data formatting | bytes 8388608
  198.5 11.8 %fusion.3 = f32[256,64,64]{2,1,0:T(8,128)S(1)} fusion(f32[256,64,64]{2,1,0:T(8,128)} %reshape.289, s32[256,64]{1,0:T(8,128)S(1)} %bitcast.83), kind=kOutput, calls=%fused_computation.21 | convolution fusion | flops 806354944 | bytes 8454144 | tf_op jit(solution)/shard_map/rsj,rst->rjt/dot_general | solution.py:65
  210.3 8.4 %fusion.2 = f32[256,64,64]{2,1,0:T(8,128)S(1)} fusion(f32[256,64,64]{2,1,0:T(8,128)S(1)} %fusion.3, s32[256,64]{1,0:T(8,128)S(1)} %bitcast.84), kind=kOutput, calls=%fused_computation.20 | convolution fusion | flops 806354944 | bytes 8454144 | tf_op jit(solution)/shard_map/rjt,rtk->rjk/dot_general | solution.py:66
  218.8 11.0 %fusion = f32[64,64,64]{2,0,1:T(8,128)} fusion(f32[256,64,64]{2,1,0:T(8,128)S(1)} %fusion.2, f32[256]{0:T(256)S(1)} %convert_element_type.50, s32[256]{0:T(256)S(1)} %eq.56), kind=kOutput, calls=%fused_computation.17 | convolution fusion | flops 805339136 | bytes 5244928 | tf_op jit(solution)/shard_map/rp,rjk->pjk/dot_general | solution.py:68
  229.8 3.0 copy.78
  232.8 1.6 gather_fusion
  235.4 1.7 broadcast_divide_fusion
  237.1 3.0 gather_fusion.4
  241.4 2.2 gather_fusion.3
  243.6 2.2 gather_fusion.1
  245.8 3.0 gather_fusion.2
  248.8 1.9 collective-permute-start.4
  251.4 39.4 %psum.63 = f32[128]{0:T(128)S(1)} all-reduce(f32[128]{0:T(128)S(1)} %fusion.6), channel_id=1, replica_groups=mesh['sector'=4,'axial'=8] {'sector','axial'}, use_global_device_ids=true, to_apply=%region_7.8 | all-reduce | flops 128 | bytes 1024 | tf_op jit(solution)/shard_map/psum | solution.py:91
  292.1 1.5 collective-permute-start.7
  294.9 1.7 collective-permute-start.5
  300.1 9.4 %collective-permute-done.5 = f32[16,64,128]{2,1,0:T(8,128)S(1)} collective-permute-done((f32[16,64,128]{2,1,0:T(8,128)S(1)}, f32[16,64,128]{2,1,0:T(8,128)S(1)}, u32[]{:S(2)}, u32[]{:S(2)}) %collective-permute-start.5) | collective-permute-done | bytes 524320 | tf_op jit(solution)/shard_map/ppermute | solution.py:17
  310.6 13.9 %multiply_reduce_fusion.4 = (f32[128]{0:T(128)S(1)}, f32[64,64,128]{2,1,0:T(8,128)}) fusion(f32[64,64,128]{2,1,0:T(8,128)S(1)} %copy-done.6, f32[64,64,128]{2,0,1:T(8,128)S(1)} %fusion.36, f32[64,64,128]{2,0,1:T(8,128)S(1)} %fusion.38, f32[64,64,128]{2,0,1:T(8,128)S(1)} %fusion.40, f32[64,64,128]{2,0,1:T(8,128)S(1)} %fusion.42, ...), kind=kOutput, calls=%fused_computation.48 | convolution fusion | flops 406847360 | bytes 13648384 | tf_op jit(solution)/shard_map/pij,pjr->pir/dot_general | solution.py:100
  324.5 14.6 %psum.64 = f32[128]{0:T(128)S(1)} all-reduce(f32[128]{0:T(128)S(1)} %get-tuple-element.16), channel_id=1, replica_groups=mesh['sector'=4,'axial'=8] {'axial'}, use_global_device_ids=true, to_apply=%region_9.10 | all-reduce | flops 128 | bytes 1024 | tf_op jit(solution)/shard_map/psum | solution.py:11
  339.1 8.4 %psum.65 = f32[128]{0:T(128)S(1)} all-reduce(f32[128]{0:T(128)S(1)} %psum.64), channel_id=1, replica_groups=mesh['sector'=4,'axial'=8] {'sector'}, use_global_device_ids=true, to_apply=%region_10.11 | all-reduce | flops 128 | bytes 1024 | tf_op jit(solution)/shard_map/psum | solution.py:12
  347.4 2.9 multiply_reduce_fusion.3
  350.3 40.7 %psum.66 = f32[128]{0:T(128)S(1)} all-reduce(f32[128]{0:T(128)S(1)} %get-tuple-element.4), channel_id=1, replica_groups=mesh['sector'=4,'axial'=8] {'sector','axial'}, use_global_device_ids=true, to_apply=%region_12.13 | all-reduce | flops 128 | bytes 1024 | tf_op jit(solution)/shard_map/psum | solution.py:91
  391.0 3.1 multiply_add_fusion.2
  394.1 3.0 gather_fusion.8
  398.4 3.0 gather_fusion.6
  401.3 1.5 collective-permute-start.8
  402.8 2.2 gather_fusion.7
  405.0 2.2 gather_fusion.5
  408.4 3.6 collective-permute-start.11
  412.0 4.3 collective-permute-done.8
  421.5 12.2 %collective-permute-done.9 = f32[16,64,128]{2,1,0:T(8,128)S(1)} collective-permute-done((f32[16,64,128]{2,1,0:T(8,128)S(1)}, f32[16,64,128]{2,1,0:T(8,128)S(1)}, u32[]{:S(2)}, u32[]{:S(2)}) %collective-permute-start.9) | collective-permute-done | bytes 524320 | tf_op jit(solution)/shard_map/ppermute | solution.py:17
  434.9 13.9 %multiply_reduce_fusion.2 = (f32[128]{0:T(128)S(1)}, f32[64,64,128]{2,1,0:T(8,128)}) fusion(f32[64,64,128]{2,1,0:T(8,128)S(1)} %copy-done.1, f32[64,64,128]{2,0,1:T(8,128)S(1)} %fusion.28, f32[64,64,128]{2,0,1:T(8,128)S(1)} %fusion.30, f32[64,64,128]{2,0,1:T(8,128)S(1)} %fusion.32, f32[64,64,128]{2,0,1:T(8,128)S(1)} %fusion.34, ...), kind=kOutput, calls=%fused_computation.44 | convolution fusion | flops 406847360 | bytes 13648384 | tf_op jit(solution)/shard_map/pij,pjr->pir/dot_general | solution.py:100
  448.8 15.3 %psum.67 = f32[128]{0:T(128)S(1)} all-reduce(f32[128]{0:T(128)S(1)} %get-tuple-element.18), channel_id=1, replica_groups=mesh['sector'=4,'axial'=8] {'axial'}, use_global_device_ids=true, to_apply=%region_14.15 | all-reduce | flops 128 | bytes 1024 | tf_op jit(solution)/shard_map/psum | solution.py:11
  464.1 9.5 %psum.68 = f32[128]{0:T(128)S(1)} all-reduce(f32[128]{0:T(128)S(1)} %psum.67), channel_id=1, replica_groups=mesh['sector'=4,'axial'=8] {'sector'}, use_global_device_ids=true, to_apply=%region_15.16 | all-reduce | flops 128 | bytes 1024 | tf_op jit(solution)/shard_map/psum | solution.py:12
  473.6 3.5 multiply_reduce_fusion.1
  477.1 38.5 %psum.69 = f32[128]{0:T(128)S(1)} all-reduce(f32[128]{0:T(128)S(1)} %get-tuple-element.2), channel_id=1, replica_groups=mesh['sector'=4,'axial'=8] {'sector','axial'}, use_global_device_ids=true, to_apply=%region_17.18 | all-reduce | flops 128 | bytes 1024 | tf_op jit(solution)/shard_map/psum | solution.py:91
  515.6 3.6 multiply_add_fusion.1
  519.1 3.0 gather_fusion.12
  523.4 3.0 gather_fusion.10
  526.4 1.5 collective-permute-start.12
  527.9 2.2 gather_fusion.11
  530.1 2.2 gather_fusion.9
  533.5 3.5 collective-permute-start.15
  537.0 4.3 collective-permute-done.12
  547.6 11.0 %collective-permute-done.13 = f32[16,64,128]{2,1,0:T(8,128)S(1)} collective-permute-done((f32[16,64,128]{2,1,0:T(8,128)S(1)}, f32[16,64,128]{2,1,0:T(8,128)S(1)}, u32[]{:S(2)}, u32[]{:S(2)}) %collective-permute-start.13) | collective-permute-done | bytes 524320 | tf_op jit(solution)/shard_map/ppermute | solution.py:17
  559.7 13.9 %multiply_reduce_fusion = (f32[128]{0:T(128)S(1)}, f32[64,64,128]{2,1,0:T(8,128)}) fusion(f32[64,64,128]{2,1,0:T(8,128)S(1)} %copy-done.5, f32[64,64,128]{2,0,1:T(8,128)S(1)} %fusion.20, f32[64,64,128]{2,0,1:T(8,128)S(1)} %fusion.22, f32[64,64,128]{2,0,1:T(8,128)S(1)} %fusion.24, f32[64,64,128]{2,0,1:T(8,128)S(1)} %fusion.26, ...), kind=kOutput, calls=%fused_computation.40 | convolution fusion | flops 406847360 | bytes 13648384 | tf_op jit(solution)/shard_map/pij,pjr->pir/dot_general | solution.py:100
  573.6 13.4 %psum.70 = f32[128]{0:T(128)S(1)} all-reduce(f32[128]{0:T(128)S(1)} %get-tuple-element.20), channel_id=1, replica_groups=mesh['sector'=4,'axial'=8] {'axial'}, use_global_device_ids=true, to_apply=%region_19.20 | all-reduce | flops 128 | bytes 1024 | tf_op jit(solution)/shard_map/psum | solution.py:11
  587.0 9.5 %psum.71 = f32[128]{0:T(128)S(1)} all-reduce(f32[128]{0:T(128)S(1)} %psum.70), channel_id=1, replica_groups=mesh['sector'=4,'axial'=8] {'sector'}, use_global_device_ids=true, to_apply=%region_20.21 | all-reduce | flops 128 | bytes 1024 | tf_op jit(solution)/shard_map/psum | solution.py:12
  596.5 5.3 multiply_subtract_fusion
  (102 shorter events, 40.7 us)
Async XLA Ops:
  5.4 14.4 %all-to-all-start.1 = ((s32[32,8,1]{1,2,0:T(1,128)}), s32[32,8,1]{1,2,0:T(1,128)S(1)}, u32[]{:S(2)}, u32[]{:S(2)}) async-start(s32[32,8,1]{1,2,0:T(1,128)} %bitcast.5), calls=%async_computation.1 | async-start | bytes 32768 | tf_op jit(solution)/shard_map/all_to_all | solution.py:60
  19.8 9.9 %all-to-all-start = ((s32[32,8,1]{1,2,0:T(1,128)}), s32[32,8,1]{1,2,0:T(1,128)S(1)}, u32[]{:S(2)}, u32[]{:S(2)}) async-start(s32[32,8,1]{1,2,0:T(1,128)} %bitcast.3), calls=%async_computation | async-start | bytes 32768 | tf_op jit(solution)/shard_map/all_to_all | solution.py:59
  22.3 5.6 copy-start.8
  29.7 47.2 %all-to-all-start.2 = ((s32[32,1,512]{2,1,0:T(1,128)}), s32[32,1,512]{2,1,0:T(1,128)S(1)}, u32[]{:S(2)}, u32[]{:S(2)}) async-start(s32[32,1,512]{2,1,0:T(1,128)} %reshape.290), calls=%async_computation.2 | async-start | bytes 131072 | tf_op jit(solution)/shard_map/all_to_all | solution.py:58
  76.9 5.9 copy-start.7
  76.9 7.7 %copy-start.10 = (s32[2,16,2]{1,2,0:T(2,128)S(1)}, s32[2,16,2]{1,2,0:T(2,128)}, u32[]{:S(2)}) copy-start(s32[2,16,2]{1,2,0:T(2,128)} %param.17) | copy-start | bytes 772
  76.9 14.9 %copy-start.9 = (f32[4096]{0:T(1024)S(1)}, f32[4096]{0:T(1024)}, u32[]{:S(2)}) copy-start(f32[4096]{0:T(1024)} %param.16) | copy-start | bytes 49156
  76.9 100.0 %all-to-all-start.3 = ((f32[32,1,32768]{2,1,0:T(1,128)}), f32[32,1,32768]{2,1,0:T(1,128)}, u32[]{:S(2)}, u32[]{:S(2)}) async-start(f32[32,1,32768]{2,1,0:T(1,128)} %reshape.288), calls=%async_computation.3 | async-start | bytes 8388608 | tf_op jit(solution)/shard_map/all_to_all | solution.py:57
  82.9 151.9 %collective-permute-start.1 = (f32[16,64]{1,0:T(8,128)S(1)}, f32[16,64]{1,0:T(8,128)S(1)}, u32[]{:S(2)}, u32[]{:S(2)}) collective-permute-start(f32[16,64]{1,0:T(8,128)S(1)} %get-tuple-element.7), channel_id=1, source_target_pairs={{0,8},{8,16},{16,24},{24,0},{1,9},{9,17},{17,25},{25,1},{2,10},{10... | collective-permute-start | bytes 12296 | tf_op jit(solution)/shard_map/ppermute | solution.py:17
  84.6 150.2 %collective-permute-start = (s32[16]{0:T(128)S(1)}, s32[16]{0:T(128)S(1)}, u32[]{:S(2)}, u32[]{:S(2)}) collective-permute-start(s32[16]{0:T(128)S(1)} %get-tuple-element.11), channel_id=1, source_target_pairs={{0,8},{8,16},{16,24},{24,0},{1,9},{9,17},{17,25},{25,1},{2,10},{10... | collective-permute-start | bytes 200 | tf_op jit(solution)/shard_map/ppermute | solution.py:17
  86.1 149.0 %collective-permute-start.3 = (f32[16,64]{1,0:T(8,128)S(1)}, f32[16,64]{1,0:T(8,128)S(1)}, u32[]{:S(2)}, u32[]{:S(2)}) collective-permute-start(f32[16,64]{1,0:T(8,128)S(1)} %get-tuple-element.6), channel_id=1, source_target_pairs={{0,1},{1,2},{2,3},{3,4},{4,5},{5,6},{6,7},{8,9},{9,10},{10,11},{11... | collective-permute-start | bytes 12296 | tf_op jit(solution)/shard_map/ppermute | solution.py:23
  87.6 4.7 collective-permute-start.2
  229.8 5.6 copy-start
  240.1 50.8 %collective-permute-start.6 = (f32[16,64,128]{2,1,0:T(8,128)}, f32[16,64,128]{2,1,0:T(8,128)}, u32[]{:S(2)}, u32[]{:S(2)}) collective-permute-start(f32[16,64,128]{2,1,0:T(8,128)} %gather_fusion.4), channel_id=1, source_target_pairs={{1,0},{2,1},{3,2},{4,3},{5,4},{6,5},{7,6},{9,8},{10,9},{11,10},{12... | collective-permute-start | bytes 1572872 | tf_op jit(solution)/shard_map/ppermute | solution.py:23
  248.8 44.8 %collective-permute-start.4 = (f32[16,64,128]{2,1,0:T(8,128)}, f32[16,64,128]{2,1,0:T(8,128)}, u32[]{:S(2)}, u32[]{:S(2)}) collective-permute-start(f32[16,64,128]{2,1,0:T(8,128)} %gather_fusion.2), channel_id=1, source_target_pairs={{0,24},{8,0},{16,8},{24,16},{1,25},{9,1},{17,9},{25,17},{2,26},{10... | collective-permute-start | bytes 1572872 | tf_op jit(solution)/shard_map/ppermute | solution.py:17
  292.1 6.8 %collective-permute-start.7 = (f32[16,64,128]{2,1,0:T(8,128)S(1)}, f32[16,64,128]{2,1,0:T(8,128)S(1)}, u32[]{:S(2)}, u32[]{:S(2)}) collective-permute-start(f32[16,64,128]{2,1,0:T(8,128)S(1)} %subtract_multiply_fusion.4), channel_id=1, source_target_pairs={{0,1},{1,2},{2,3},{3,4},{4,5},{5,6},{6,7},{8,9},{9,10},{10,11},{11... | collective-permute-start | bytes 1572872 | tf_op jit(solution)/shard_map/ppermute | solution.py:23
  294.9 14.6 %collective-permute-start.5 = (f32[16,64,128]{2,1,0:T(8,128)S(1)}, f32[16,64,128]{2,1,0:T(8,128)S(1)}, u32[]{:S(2)}, u32[]{:S(2)}) collective-permute-start(f32[16,64,128]{2,1,0:T(8,128)S(1)} %subtract_multiply_fusion.5), channel_id=1, source_target_pairs={{0,8},{8,16},{16,24},{24,0},{1,9},{9,17},{17,25},{25,1},{2,10},{10... | collective-permute-start | bytes 1572872 | tf_op jit(solution)/shard_map/ppermute | solution.py:17
  298.9 11.7 %copy-start.2 = (f32[64,64,64]{2,0,1:T(8,128)S(1)}, f32[64,64,64]{2,0,1:T(8,128)}, u32[]{:S(2)}) copy-start(f32[64,64,64]{2,0,1:T(8,128)} %fusion) | copy-start | bytes 3145732
  298.9 11.7 %copy-start.6 = (f32[64,64,128]{2,1,0:T(8,128)S(1)}, f32[64,64,128]{2,1,0:T(8,128)}, u32[]{:S(2)}) copy-start(f32[64,64,128]{2,1,0:T(8,128)} %broadcast_divide_fusion) | copy-start | bytes 6291460
  397.1 10.1 %collective-permute-start.10 = (f32[16,64,128]{2,1,0:T(8,128)}, f32[16,64,128]{2,1,0:T(8,128)}, u32[]{:S(2)}, u32[]{:S(2)}) collective-permute-start(f32[16,64,128]{2,1,0:T(8,128)} %gather_fusion.8), channel_id=1, source_target_pairs={{1,0},{2,1},{3,2},{4,3},{5,4},{6,5},{7,6},{9,8},{10,9},{11,10},{12... | collective-permute-start | bytes 1572872 | tf_op jit(solution)/shard_map/ppermute | solution.py:23
  401.3 15.0 %collective-permute-start.8 = (f32[16,64,128]{2,1,0:T(8,128)}, f32[16,64,128]{2,1,0:T(8,128)}, u32[]{:S(2)}, u32[]{:S(2)}) collective-permute-start(f32[16,64,128]{2,1,0:T(8,128)} %gather_fusion.6), channel_id=1, source_target_pairs={{0,24},{8,0},{16,8},{24,16},{1,25},{9,1},{17,9},{25,17},{2,26},{10... | collective-permute-start | bytes 1572872 | tf_op jit(solution)/shard_map/ppermute | solution.py:17
  408.4 11.9 %collective-permute-start.11 = (f32[16,64,128]{2,1,0:T(8,128)S(1)}, f32[16,64,128]{2,1,0:T(8,128)S(1)}, u32[]{:S(2)}, u32[]{:S(2)}) collective-permute-start(f32[16,64,128]{2,1,0:T(8,128)S(1)} %subtract_multiply_fusion.2), channel_id=1, source_target_pairs={{0,1},{1,2},{2,3},{3,4},{4,5},{5,6},{6,7},{8,9},{9,10},{10,11},{11... | collective-permute-start | bytes 1572872 | tf_op jit(solution)/shard_map/ppermute | solution.py:23
  417.5 16.2 %collective-permute-start.9 = (f32[16,64,128]{2,1,0:T(8,128)S(1)}, f32[16,64,128]{2,1,0:T(8,128)S(1)}, u32[]{:S(2)}, u32[]{:S(2)}) collective-permute-start(f32[16,64,128]{2,1,0:T(8,128)S(1)} %subtract_multiply_fusion.3), channel_id=1, source_target_pairs={{0,8},{8,16},{16,24},{24,0},{1,9},{9,17},{17,25},{25,1},{2,10},{10... | collective-permute-start | bytes 1572872 | tf_op jit(solution)/shard_map/ppermute | solution.py:17
  420.3 14.6 %copy-start.1 = (f32[64,64,128]{2,1,0:T(8,128)S(1)}, f32[64,64,128]{2,1,0:T(8,128)}, u32[]{:S(2)}) copy-start(f32[64,64,128]{2,1,0:T(8,128)} %multiply_add_fusion.2) | copy-start | bytes 6291460
  420.3 14.6 %copy-start.3 = (f32[64,64,64]{2,0,1:T(8,128)S(1)}, f32[64,64,64]{2,0,1:T(8,128)}, u32[]{:S(2)}) copy-start(f32[64,64,64]{2,0,1:T(8,128)} %fusion) | copy-start | bytes 3145732
  522.1 10.2 %collective-permute-start.14 = (f32[16,64,128]{2,1,0:T(8,128)}, f32[16,64,128]{2,1,0:T(8,128)}, u32[]{:S(2)}, u32[]{:S(2)}) collective-permute-start(f32[16,64,128]{2,1,0:T(8,128)} %gather_fusion.12), channel_id=1, source_target_pairs={{1,0},{2,1},{3,2},{4,3},{5,4},{6,5},{7,6},{9,8},{10,9},{11,10},{12... | collective-permute-start | bytes 1572872 | tf_op jit(solution)/shard_map/ppermute | solution.py:23
  526.4 15.0 %collective-permute-start.12 = (f32[16,64,128]{2,1,0:T(8,128)}, f32[16,64,128]{2,1,0:T(8,128)}, u32[]{:S(2)}, u32[]{:S(2)}) collective-permute-start(f32[16,64,128]{2,1,0:T(8,128)} %gather_fusion.10), channel_id=1, source_target_pairs={{0,24},{8,0},{16,8},{24,16},{1,25},{9,1},{17,9},{25,17},{2,26},{10... | collective-permute-start | bytes 1572872 | tf_op jit(solution)/shard_map/ppermute | solution.py:17
  533.5 12.8 %collective-permute-start.15 = (f32[16,64,128]{2,1,0:T(8,128)S(1)}, f32[16,64,128]{2,1,0:T(8,128)S(1)}, u32[]{:S(2)}, u32[]{:S(2)}) collective-permute-start(f32[16,64,128]{2,1,0:T(8,128)S(1)} %subtract_multiply_fusion), channel_id=1, source_target_pairs={{0,1},{1,2},{2,3},{3,4},{4,5},{5,6},{6,7},{8,9},{9,10},{10,11},{11... | collective-permute-start | bytes 1572872 | tf_op jit(solution)/shard_map/ppermute | solution.py:23
  542.6 16.0 %collective-permute-start.13 = (f32[16,64,128]{2,1,0:T(8,128)S(1)}, f32[16,64,128]{2,1,0:T(8,128)S(1)}, u32[]{:S(2)}, u32[]{:S(2)}) collective-permute-start(f32[16,64,128]{2,1,0:T(8,128)S(1)} %subtract_multiply_fusion.1), channel_id=1, source_target_pairs={{0,8},{8,16},{16,24},{24,0},{1,9},{9,17},{17,25},{25,1},{2,10},{10... | collective-permute-start | bytes 1572872 | tf_op jit(solution)/shard_map/ppermute | solution.py:17
  546.4 13.4 %copy-start.4 = (f32[64,64,64]{2,0,1:T(8,128)S(1)}, f32[64,64,64]{2,0,1:T(8,128)}, u32[]{:S(2)}) copy-start(f32[64,64,64]{2,0,1:T(8,128)} %fusion) | copy-start | bytes 3145732
  546.4 13.3 %copy-start.5 = (f32[64,64,128]{2,1,0:T(8,128)S(1)}, f32[64,64,128]{2,1,0:T(8,128)}, u32[]{:S(2)}) copy-start(f32[64,64,128]{2,1,0:T(8,128)} %multiply_add_fusion.1) | copy-start | bytes 6291460
